TPU v7x, 512 devices: a whole 4x4x16 slice. The times are simulated.
512 devices in a mesh: band: 16 (over x, y), region: 32 (over z, core).
Axes of the slice: x: 4, y: 4, z: 16, core: 2. Of those that a mesh axis runs over, the one named last changes fastest.
Arguments:
- state: bfloat16 [16, 32768], P(None, 'region'), may hold values from -4 to 4
- absorb_weight: bfloat16 [16, 16384], P(None, 'band'), may hold values from -1.5 to 1.5
- emit_weight: bfloat16 [16, 16384], P(None, 'band'), may hold values from -1.5 to 1.5
- path_len: float32 [8, 8192], P(None, 'region'), may hold values from 0.02 to 0.2
- crossing_slot: int32 [8, 8192], P(None, 'region'), may hold values from 0 to 4095, as said below
- request_rows: int32 [32, 32, 128], P('region'), may hold values from 0 to 1023
- cot_intensity: float32 [16384, 8192], P('band', 'region'), may hold values from -6 to 6
Outputs:
- grad_state: float32 [16, 32768], P(None, 'region')
Inputs may be any that keep to these rules, and one draw needn't show every extreme that they name: `crossing_slot`: within each ray block (the 256 rays of one index of region) the 2048 crossings take distinct slots; slot p * 128 + s names the cell listed at request_rows[block, p, s]. In every draw one region has all 128 of its slots taken by every ray block; the other listed slots are partly unused.
All inputs are finite; a program needn't handle non-finite values.
Results may differ from a plain program's by a relative error of at most 0.0051.
Values may be sent and summed in bfloat16 or wider, within the bound.
No kernel may reach another device: no remote copies, remote signals or barrier semaphores. Data moves between devices by JAX's collectives and lax.ppermute only.
A program may use at most 64 MiB of HBM per device.

v0:
```python
import jax
import jax.numpy as jnp
from jax import lax
from jax.sharding import PartitionSpec as P


def adjoint_block(absorb_x, emit_x, length, cot_block, w_abs, w_emit):
    depth_step = absorb_x.astype(jnp.float32) * length[None]
    passed = jnp.cumsum(depth_step, axis=1) - depth_step
    transmit = jnp.exp(-passed)
    emitted = emit_x.astype(jnp.float32) * length[None] * transmit
    behind = lax.cumsum(emitted, axis=1, reverse=True) - emitted
    grad_emit = (cot_block[:, None, :] * emitted).astype(jnp.bfloat16)
    grad_absorb = (-cot_block[:, None, :] * depth_step * behind).astype(jnp.bfloat16)
    bin_count = grad_emit.shape[0]
    grad_emit = grad_emit.reshape(bin_count, -1)
    grad_absorb = grad_absorb.reshape(bin_count, -1)
    return jnp.dot(w_abs, grad_absorb, preferred_element_type=jnp.float32) + jnp.dot(
        w_emit, grad_emit, preferred_element_type=jnp.float32
    )


def on_device(
    state, absorb_weight, emit_weight, path_len, crossing_slot, request_rows, cot_intensity
):
    bin_count = absorb_weight.shape[1]
    state_count = state.shape[0]
    cross_len = path_len.shape[0]
    ray_count = path_len.shape[1]
    wanted = lax.all_to_all(
        request_rows, "region", split_axis=1, concat_axis=0, tiled=True
    ).reshape(-1)
    slot_ids = crossing_slot.reshape(-1)
    picked = jnp.take(state, wanted, axis=1)
    arrived = lax.all_to_all(picked, "region", split_axis=1, concat_axis=1, tiled=True)
    state_x = jnp.take(arrived, slot_ids, axis=1)
    absorb_x = jnp.exp(
        jnp.dot(absorb_weight.T, state_x, preferred_element_type=jnp.float32)
    ).astype(jnp.bfloat16)
    emit_x = jnp.exp(jnp.dot(emit_weight.T, state_x, preferred_element_type=jnp.float32)).astype(
        jnp.bfloat16
    )
    bin_block = 256
    summed = jnp.zeros((state_count, cross_len * ray_count), jnp.float32)
    for first_bin in range(0, bin_count, bin_block):
        last_bin = first_bin + bin_block
        summed = summed + adjoint_block(
            absorb_x[first_bin:last_bin].reshape(bin_block, cross_len, ray_count),
            emit_x[first_bin:last_bin].reshape(bin_block, cross_len, ray_count),
            path_len,
            cot_intensity[first_bin:last_bin],
            absorb_weight[:, first_bin:last_bin],
            emit_weight[:, first_bin:last_bin],
        )
    sending = jnp.zeros((state_count, wanted.shape[0]), jnp.float32).at[:, slot_ids].set(summed)
    returned = lax.all_to_all(sending, "region", split_axis=1, concat_axis=1, tiled=True)
    partial_value = (
        jnp.zeros((state_count, state.shape[1]), jnp.float32).at[:, wanted].add(returned)
    )
    partial_value = lax.psum(partial_value, "band")
    return partial_value


def solution(mesh):
    return jax.shard_map(
        on_device,
        mesh=mesh,
        in_specs=(
            P(None, "region"),
            P(None, "band"),
            P(None, "band"),
            P(None, "region"),
            P(None, "region"),
            P("region", None, None),
            P("band", "region"),
        ),
        out_specs=P(None, "region"),
        check_vma=False,
    )
```

profile of v0, /device:TPU:32, one launch (start us, length us, event | category | flops | bytes accessed | tf_op | source)
XLA Modules:
  0.0 268.6 jit_solution(6498890352738340585)
XLA Ops:
  6.5 15.5 %all-to-all-start = ((s32[1,32,128]{2,0,1:T(1,128)}), s32[1,32,128]{2,0,1:T(1,128)S(1)}, u32[]{:S(2)}, u32[]{:S(2)}) async-start(s32[1,32,128]{2,0,1:T(1,128)} %bitcast.180), calls=%async_computation | async-start | bytes 32768 | tf_op jit(solution)/shard_map/all_to_all | solution.py:30
  22.0 0.7 copy.52
  22.7 0.6 compare_select_fusion.1
  23.3 0.9 copy.36
  24.3 8.9 %all-to-all-done = s32[1,32,128]{2,0,1:T(1,128)S(1)} async-done(((s32[1,32,128]{2,0,1:T(1,128)}), s32[1,32,128]{2,0,1:T(1,128)S(1)}, u32[]{:S(2)}, u32[]{:S(2)}) %all-to-all-start) | async-done | bytes 16416 | tf_op jit(solution)/shard_map/all_to_all | solution.py:30
  33.2 0.0 copy-start.5
  33.2 0.6 copy-done.5
  33.8 12.1 %gather_fusion = bf16[4096,16]{1,0:T(8,128)(2,1)S(1)} fusion(bf16[16,1024]{0,1:T(8,128)(2,1)S(1)} %copy.36, s32[4096]{0:T(1024)S(1)} %broadcast_clamp_fusion), kind=kCustom, calls=%fused_computation | custom fusion | bytes 278528 | tf_op jit(solution)/shard_map/jit(_take)/gather | solution.py:34
  46.0 0.3 copy.37
  46.3 0.0 copy-start.6
  46.3 0.7 broadcast_select_fusion.3
  47.0 5.0 %all-to-all-start.1 = ((bf16[16,32,128]{2,0,1:T(8,128)(2,1)}), bf16[16,32,128]{2,0,1:T(8,128)(2,1)S(1)}, u32[]{:S(2)}, u32[]{:S(2)}) async-start(bf16[16,32,128]{2,0,1:T(8,128)(2,1)} %broadcast_select_fusion.3), calls=%async_computation.1 | async-start | bytes 262144 | tf_op jit(solution)/shard_map/all_to_all | solution.py:35
  52.0 0.0 all-reduce.2.cloned.1.call-start
  52.0 0.0 copy-done.1
  52.0 0.2 fusion.91
  52.2 0.0 copy-done.2
  52.2 0.0 copy-done.6
  52.3 0.0 copy-start.7
  52.3 0.1 copy.45
  52.4 0.1 copy.35
  52.5 0.1 copy.40
  52.7 0.1 copy.42
  52.8 0.1 copy.44
  53.0 0.1 copy.41
  53.1 0.1 copy.39
  53.2 0.8 copy.43
  54.1 0.6 compare_and_fusion.1
  54.7 0.6 broadcast_clamp_fusion.1
  55.2 12.8 %all-to-all-done.1 = bf16[16,32,128]{2,0,1:T(8,128)(2,1)S(1)} async-done(((bf16[16,32,128]{2,0,1:T(8,128)(2,1)}), bf16[16,32,128]{2,0,1:T(8,128)(2,1)S(1)}, u32[]{:S(2)}, u32[]{:S(2)}) %all-to-all-start.1) | async-done | bytes 131104 | tf_op jit(solution)/shard_map/all_to_all | solution.py:35
  68.1 0.5 copy.38
  68.6 7.3 %gather_fusion.1 = bf16[2048,16]{1,0:T(8,128)(2,1)S(1)} fusion(bf16[16,4096]{0,1:T(8,128)(2,1)S(1)} %bitcast.166, s32[2048]{0:T(1024)} %broadcast_clamp_fusion.1), kind=kCustom, calls=%fused_computation.1 | custom fusion | bytes 139264 | tf_op jit(solution)/shard_map/jit(_take)/gather | solution.py:36
  75.9 0.0 copy-start.4
  75.9 2.4 fusion
  78.4 1.6 fusion.1
  80.0 0.7 slice_convert_fusion
  80.7 0.7 slice_convert_fusion.1
  81.4 0.3 fusion.57
  81.7 0.3 fusion.54
  82.1 0.9 fusion.35
  83.0 0.9 fusion.29
  83.9 0.0 copy-done
  84.0 2.5 fusion.5
  86.5 0.4 fusion.78
  86.9 0.4 fusion.81
  87.3 0.4 fusion.60
  87.7 0.3 fusion.63
  88.0 0.9 fusion.41
  89.0 0.9 fusion.47
  89.8 2.6 fusion.17
  92.5 0.4 fusion.84
  92.9 0.4 fusion.87
  93.2 0.4 convolution_add_fusion.3
  93.6 0.4 fusion.4
  94.0 0.4 fusion.3
  94.4 0.4 fusion.2
  94.8 0.3 copy.46
  95.2 6.2 %scatter_custom_fusion = f32[16,4096]{0,1:T(8,128)S(1)} fusion(s32[2048]{0:T(1024)} %bitcast.177, f32[2048,16]{1,0:T(8,128)S(1)} %copy.46, f32[]{:T(128)} %constant.41.clone.1), kind=kCustom, calls=%fused_computation.107 | custom fusion | bytes 262656 | tf_op jit(solution)/shard_map/scatter | solution.py:55
  101.4 0.6 copy.47
  102.0 25.2 %all_to_all.30 = f32[16,32,128]{2,0,1:T(8,128)S(1)} all-to-all(f32[16,32,128]{2,0,1:T(8,128)S(1)} %copy.47), channel_id=1, replica_groups=mesh['band'=16,'region'=32] {'region'}, dimensions={1} | all-to-all | bytes 524288 | tf_op jit(solution)/shard_map/all_to_all | solution.py:56
  127.1 0.6 copy.49
  127.8 23.3 %scatter_custom_fusion.1 = f32[16,1024]{0,1:T(8,128)} fusion(s32[4096]{0:T(1024)} %bitcast.173, f32[4096,16]{1,0:T(8,128)S(1)} %copy.49, f32[]{:T(128)} %constant.41.clone.1), kind=kCustom, calls=%fused_computation.111 | custom fusion | flops 65536 | bytes 66048 | tf_op jit(solution)/shard_map/scatter-add | solution.py:58
  151.0 0.0 all-reduce.2.cloned.1.call-update
  151.0 108.9 %all-reduce.2.cloned.1.call-done = f32[16,1024]{0,1:T(8,128)} async-done(((f32[16,1024]{0,1:T(8,128)}), f32[16,1024]{0,1:T(8,128)}) %all-reduce.2.cloned.1.call-update) | async-done | bytes 65552 | tf_op jit(solution)/shard_map/psum | solution.py:60
  259.9 1.8 copy.50
  (15 shorter events, 0.1 us)
Async XLA Ops:
  6.5 45.5 %copy-start.1 = (f32[1024,256]{1,0:T(8,128)S(1)}, f32[1024,256]{1,0:T(8,128)}, u32[]{:S(2)}) copy-start(f32[1024,256]{1,0:T(8,128)} %param.13) | copy-start | bytes 3145732
  6.5 26.7 %all-to-all-start = ((s32[1,32,128]{2,0,1:T(1,128)}), s32[1,32,128]{2,0,1:T(1,128)S(1)}, u32[]{:S(2)}, u32[]{:S(2)}) async-start(s32[1,32,128]{2,0,1:T(1,128)} %bitcast.180), calls=%async_computation | async-start | bytes 32768 | tf_op jit(solution)/shard_map/all_to_all | solution.py:30
  33.2 0.6 copy-start.5
  46.3 5.9 %copy-start.2 = (f32[8,256]{1,0:T(8,128)S(1)}, f32[8,256]{1,0:T(8,128)}, u32[]{:S(2)}) copy-start(f32[8,256]{1,0:T(8,128)} %param.10) | copy-start | bytes 24580
  46.3 5.9 %copy-start.6 = (s32[8,256]{1,0:T(8,128)S(1)}, s32[8,256]{1,0:T(8,128)}, u32[]{:S(2)}) copy-start(s32[8,256]{1,0:T(8,128)} %param.11) | copy-start | bytes 24580
  47.0 21.1 %all-to-all-start.1 = ((bf16[16,32,128]{2,0,1:T(8,128)(2,1)}), bf16[16,32,128]{2,0,1:T(8,128)(2,1)S(1)}, u32[]{:S(2)}, u32[]{:S(2)}) async-start(bf16[16,32,128]{2,0,1:T(8,128)(2,1)} %broadcast_select_fusion.3), calls=%async_computation.1 | async-start | bytes 262144 | tf_op jit(solution)/shard_map/all_to_all | solution.py:35
  52.0 207.9 %all-reduce.2.cloned.1.call-start = ((), (), s32[]{:S(2)}) async-start(), calls=%async_computation.3 | async-start | bytes 1048576 | tf_op jit(solution)/shard_map/psum | solution.py:60
  52.3 2.4 copy-start.7
  75.9 2.4 copy-start.4
  75.9 2.4 copy-start.8
  83.0 1.0 copy-start
  84.0 2.6 copy-start.3
Sparse Core Ops, SparseCore 0:
  151.2 108.6 all-reduce.1
where the time goes:
time: 269 us
  waiting for transfers between devices  131 us (49%)
  other arithmetic  37.5 us (14%)
  local copies, waits for them, and re-layouts  33.9 us (13%)
  blocking collectives  25.2 us (9%)
  starting transfers between devices  20.5 us (8%)
  between operations  13.8 us (5%)
  matrix products  7.06 us (3%)
    psum x1, waiting for transfers between devices, on_device(): partial_value = lax.psum(partial_value, 'band')  109 us
    all_to_all x1, blocking collectives, on_device(): lax.all_to_all(sending, 'region', split_axis=1, concat_axis=1, tiled=True)  25.2 us
    scatter-add x1, other arithmetic, on_device(): jnp.zeros((state_count, state.shape[1]), jnp.float32).at[:, wanted]  23.3 us
    all_to_all x1, starting transfers between devices, on_device(): lax.all_to_all(request_rows, 'region', split_axis=1, concat_axis=0, tiled...  15.5 us
    all_to_all x1, waiting for transfers between devices, on_device(): lax.all_to_all(picked, 'region', split_axis=1, concat_axis=1, tiled=True)  12.8 us
    gather x2, local copies, waits for them, and re-layouts, on_device(): picked = jnp.take(state, wanted, axis=1)  12.5 us
    all_to_all x1, waiting for transfers between devices, on_device(): lax.all_to_all(request_rows, 'region', split_axis=1, concat_axis=0, tiled...  8.92 us
    gather x1, local copies, waits for them, and re-layouts, on_device(): state_x = jnp.take(arrived, slot_ids, axis=1)  7.34 us
  transfers between devices with their start and end apart: 3, of which 3 were waited for; matrix products, arithmetic and copies ran while one was open for 2% of the time, Pallas kernels for 0%

commit v1 on v0

--- a/solution.py
+++ b/solution.py
@@ -57,7 +57,7 @@
     partial_value = (
         jnp.zeros((state_count, state.shape[1]), jnp.float32).at[:, wanted].add(returned)
     )
-    partial_value = lax.psum(partial_value, "band")
+    partial_value = jnp.sum(lax.all_gather(partial_value, "band"), axis=0)
     return partial_value
 
 

time: 269 us -> 212 us (0.79)
  waiting for transfers between devices: 131 us -> 72.7 us
    psum x1 -> x0, waiting for transfers between devices: 109 us -> none  [on_device(): partial_value = lax.psum(partial_value, 'band')]
    all_gather x0 -> x1, waiting for transfers between devices: none -> 51 us  [on_device(): partial_value = jnp.sum(lax.all_gather(partial_value, 'band'), axis=0)]
  transfers between devices with their start and end apart: 3 -> 3, of which waited for: 3 -> 3; matrix products, arithmetic and copies ran while one was open for 2% -> 3% of each run, Pallas kernels for 0% -> 0%
where the time goes in v1:
time: 212 us; the launch traced here: 211 us
  waiting for transfers between devices  72.7 us (34%)
  other arithmetic  38.8 us (18%)
  local copies, waits for them, and re-layouts  32.9 us (16%)
  blocking collectives  25.2 us (12%)
  starting transfers between devices  20.5 us (10%)
  between operations  13.8 us (7%)
  matrix products  7.06 us (3%)
    all_gather x1, waiting for transfers between devices, on_device(): partial_value = jnp.sum(lax.all_gather(partial_value, 'band'), axis=0)  51 us
    all_to_all x1, blocking collectives, on_device(): lax.all_to_all(sending, 'region', split_axis=1, concat_axis=1, tiled=True)  25.2 us
    scatter-add x1, other arithmetic, on_device(): jnp.zeros((state_count, state.shape[1]), jnp.float32).at[:, wanted]  22.6 us
    all_to_all x1, starting transfers between devices, on_device(): lax.all_to_all(request_rows, 'region', split_axis=1, concat_axis=0, tiled...  15.5 us
    all_to_all x1, waiting for transfers between devices, on_device(): lax.all_to_all(picked, 'region', split_axis=1, concat_axis=1, tiled=True)  12.8 us
    gather x2, local copies, waits for them, and re-layouts, on_device(): picked = jnp.take(state, wanted, axis=1)  12.5 us
    all_to_all x1, waiting for transfers between devices, on_device(): lax.all_to_all(request_rows, 'region', split_axis=1, concat_axis=0, tiled...  8.92 us
    gather x1, local copies, waits for them, and re-layouts, on_device(): state_x = jnp.take(arrived, slot_ids, axis=1)  7.34 us
  transfers between devices with their start and end apart: 3, of which 3 were waited for; matrix products, arithmetic and copies ran while one was open for 3% of the time, Pallas kernels for 0%

profile of v1, /device:TPU:32, one launch (start us, length us, event | category | flops | bytes accessed | tf_op | source)
XLA Modules:
  0.0 210.9 jit_solution(7667626402702220105)
XLA Ops:
  6.5 15.5 %all-to-all-start = ((s32[1,32,128]{2,0,1:T(1,128)}), s32[1,32,128]{2,0,1:T(1,128)S(1)}, u32[]{:S(2)}, u32[]{:S(2)}) async-start(s32[1,32,128]{2,0,1:T(1,128)} %bitcast.182), calls=%async_computation | async-start | bytes 32768 | tf_op jit(solution)/shard_map/all_to_all | solution.py:30
  22.0 0.7 copy.62
  22.7 0.6 compare_select_fusion.1
  23.3 0.9 copy.46
  24.3 8.9 %all-to-all-done = s32[1,32,128]{2,0,1:T(1,128)S(1)} async-done(((s32[1,32,128]{2,0,1:T(1,128)}), s32[1,32,128]{2,0,1:T(1,128)S(1)}, u32[]{:S(2)}, u32[]{:S(2)}) %all-to-all-start) | async-done | bytes 16416 | tf_op jit(solution)/shard_map/all_to_all | solution.py:30
  33.2 0.0 copy-start.5
  33.2 0.6 copy-done.5
  33.8 12.1 %gather_fusion = bf16[4096,16]{1,0:T(8,128)(2,1)S(1)} fusion(bf16[16,1024]{0,1:T(8,128)(2,1)S(1)} %copy.46, s32[4096]{0:T(1024)S(1)} %broadcast_clamp_fusion), kind=kCustom, calls=%fused_computation | custom fusion | bytes 278528 | tf_op jit(solution)/shard_map/jit(_take)/gather | solution.py:34
  46.0 0.3 copy.47
  46.3 0.0 copy-start.6
  46.3 0.7 broadcast_select_fusion.3
  47.0 5.0 %all-to-all-start.1 = ((bf16[16,32,128]{2,0,1:T(8,128)(2,1)}), bf16[16,32,128]{2,0,1:T(8,128)(2,1)S(1)}, u32[]{:S(2)}, u32[]{:S(2)}) async-start(bf16[16,32,128]{2,0,1:T(8,128)(2,1)} %broadcast_select_fusion.3), calls=%async_computation.1 | async-start | bytes 262144 | tf_op jit(solution)/shard_map/all_to_all | solution.py:35
  52.0 0.0 all-gather.3.cloned.1.call-start
  52.0 0.0 copy-done.1
  52.0 0.2 fusion.91
  52.3 0.0 copy-start.7
  52.3 0.1 copy.55
  52.4 0.1 copy.45
  52.5 0.1 copy.50
  52.7 0.1 copy.52
  52.8 0.1 copy.54
  53.0 0.1 copy.51
  53.1 0.1 copy.49
  53.2 0.8 copy.53
  54.1 0.6 compare_and_fusion.1
  54.7 0.0 copy-done.7
  54.7 0.6 broadcast_clamp_fusion.1
  55.2 12.8 %all-to-all-done.1 = bf16[16,32,128]{2,0,1:T(8,128)(2,1)S(1)} async-done(((bf16[16,32,128]{2,0,1:T(8,128)(2,1)}), bf16[16,32,128]{2,0,1:T(8,128)(2,1)S(1)}, u32[]{:S(2)}, u32[]{:S(2)}) %all-to-all-start.1) | async-done | bytes 131104 | tf_op jit(solution)/shard_map/all_to_all | solution.py:35
  68.1 0.5 copy.48
  68.6 7.3 %gather_fusion.1 = bf16[2048,16]{1,0:T(8,128)(2,1)S(1)} fusion(bf16[16,4096]{0,1:T(8,128)(2,1)S(1)} %bitcast.167, s32[2048]{0:T(1024)} %broadcast_clamp_fusion.1), kind=kCustom, calls=%fused_computation.1 | custom fusion | bytes 139264 | tf_op jit(solution)/shard_map/jit(_take)/gather | solution.py:36
  75.9 0.0 copy-start.4
  75.9 2.4 %fusion = bf16[1024,2048]{0,1:T(8,128)(2,1)S(1)} fusion(bf16[16,1024]{1,0:T(8,128)(2,1)} %param.8, bf16[2048,16]{1,0:T(8,128)(2,1)S(1)} %gather_fusion.1, pred[2048]{0:T(1024)(128)(4,1)} %compare_and_fusion.1), kind=kOutput, calls=%fused_computation.6 | convolution fusion | flops 69238784 | bytes 4294656 | tf_op jit(solution)/shard_map/dot_general | solution.py:38
  78.4 1.6 fusion.1
  80.0 0.7 slice_convert_fusion
  80.7 0.7 slice_convert_fusion.1
  81.4 0.3 fusion.57
  81.7 0.3 fusion.54
  82.1 0.9 fusion.35
  83.0 0.9 fusion.29
  83.9 0.0 copy-done
  84.0 2.5 %fusion.5 = (bf16[256,2048]{0,1:T(8,128)(2,1)S(1)}, bf16[256,2048]{0,1:T(8,128)(2,1)S(1)}, bf16[256,2048]{0,1:T(8,128)(2,1)S(1)}, bf16[256,2048]{0,1:T(8,128)(2,1)S(1)}) fusion(f32[256,256]{0,1:T(8,128)S(1)} %copy.55, bf16[1024,2048]{0,1:T(8,128)(2,1)S(1)} %fusion, f32[256,8,256]{0,2,1:T(8,128)S(1)} %fusion.54, f32[2048]{0:T(1024)S(1)} %bitcast.172, ...), kind=kLoop, calls=%fused_computation.16 | loop fusion | flops 13631488 | bytes 17833984 | tf_op jit(solution)/shard_map/convert_element_type | solution.py:13
  86.5 0.4 fusion.78
  86.9 0.4 fusion.81
  87.3 0.4 fusion.60
  87.7 0.3 fusion.63
  88.0 0.9 fusion.41
  89.0 0.9 fusion.47
  89.8 2.6 %fusion.17 = (bf16[256,2048]{0,1:T(8,128)(2,1)S(1)}, bf16[256,2048]{0,1:T(8,128)(2,1)S(1)}, bf16[256,2048]{0,1:T(8,128)(2,1)S(1)}, bf16[256,2048]{0,1:T(8,128)(2,1)S(1)}) fusion(f32[256,256]{0,1:T(8,128)S(1)} %copy.51, bf16[1024,2048]{0,1:T(8,128)(2,1)S(1)} %fusion, f32[256,8,256]{0,2,1:T(8,128)S(1)} %fusion.60, f32[2048]{0:T(1024)S(1)} %bitcast.173, ...), kind=kLoop, calls=%fused_computation.36 | loop fusion | flops 13631488 | bytes 17833984 | tf_op jit(solution)/shard_map/convert_element_type | solution.py:13
  92.5 0.4 fusion.84
  92.9 0.4 fusion.87
  93.2 0.4 convolution_add_fusion.3
  93.6 0.4 fusion.4
  94.0 0.4 fusion.3
  94.4 0.4 fusion.2
  94.8 0.3 copy.56
  95.2 6.2 %scatter_custom_fusion = f32[16,4096]{0,1:T(8,128)S(1)} fusion(s32[2048]{0:T(1024)} %bitcast.179, f32[2048,16]{1,0:T(8,128)S(1)} %copy.56, f32[]{:T(128)} %constant.42.clone.1), kind=kCustom, calls=%fused_computation.107 | custom fusion | bytes 262656 | tf_op jit(solution)/shard_map/scatter | solution.py:55
  101.4 0.6 copy.57
  102.0 25.2 %all_to_all.30 = f32[16,32,128]{2,0,1:T(8,128)S(1)} all-to-all(f32[16,32,128]{2,0,1:T(8,128)S(1)} %copy.57), channel_id=1, replica_groups=mesh['band'=16,'region'=32] {'region'}, dimensions={1} | all-to-all | bytes 524288 | tf_op jit(solution)/shard_map/all_to_all | solution.py:56
  127.1 0.6 copy.59
  127.8 22.6 %scatter_custom_fusion.1 = f32[16,1024]{0,1:T(8,128)S(1)} fusion(s32[4096]{0:T(1024)} %bitcast.175, f32[4096,16]{1,0:T(8,128)S(1)} %copy.59, f32[]{:T(128)} %constant.42.clone.1), kind=kCustom, calls=%fused_computation.111 | custom fusion | flops 65536 | bytes 66048 | tf_op jit(solution)/shard_map/scatter-add | solution.py:58
  150.4 0.8 copy.60
  151.2 0.0 all-gather.3.cloned.1.call-update
  151.2 51.0 %all-gather.3.cloned.1.call-done = f32[256,1024]{1,0:T(8,128)} async-done(((f32[16,1024]{1,0:T(8,128)}), f32[256,1024]{1,0:T(8,128)}) %all-gather.3.cloned.1.call-update) | async-done | bytes 1048592 | tf_op jit(solution)/shard_map/all_gather | solution.py:60
  202.2 1.9 reduce_sum.9
  (16 shorter events, 0.1 us)
Async XLA Ops:
  6.5 45.5 %copy-start.1 = (f32[1024,256]{1,0:T(8,128)S(1)}, f32[1024,256]{1,0:T(8,128)}, u32[]{:S(2)}) copy-start(f32[1024,256]{1,0:T(8,128)} %param.13) | copy-start | bytes 3145732
  6.5 26.7 %all-to-all-start = ((s32[1,32,128]{2,0,1:T(1,128)}), s32[1,32,128]{2,0,1:T(1,128)S(1)}, u32[]{:S(2)}, u32[]{:S(2)}) async-start(s32[1,32,128]{2,0,1:T(1,128)} %bitcast.182), calls=%async_computation | async-start | bytes 32768 | tf_op jit(solution)/shard_map/all_to_all | solution.py:30
  33.2 0.6 copy-start.5
  46.3 5.9 %copy-start.2 = (f32[8,256]{1,0:T(8,128)S(1)}, f32[8,256]{1,0:T(8,128)}, u32[]{:S(2)}) copy-start(f32[8,256]{1,0:T(8,128)} %param.10) | copy-start | bytes 24580
  46.3 5.9 %copy-start.6 = (s32[8,256]{1,0:T(8,128)S(1)}, s32[8,256]{1,0:T(8,128)}, u32[]{:S(2)}) copy-start(s32[8,256]{1,0:T(8,128)} %param.11) | copy-start | bytes 24580
  47.0 21.1 %all-to-all-start.1 = ((bf16[16,32,128]{2,0,1:T(8,128)(2,1)}), bf16[16,32,128]{2,0,1:T(8,128)(2,1)S(1)}, u32[]{:S(2)}, u32[]{:S(2)}) async-start(bf16[16,32,128]{2,0,1:T(8,128)(2,1)} %broadcast_select_fusion.3), calls=%async_computation.1 | async-start | bytes 262144 | tf_op jit(solution)/shard_map/all_to_all | solution.py:35
  52.0 150.2 %all-gather.3.cloned.1.call-start = ((), (), s32[]{:S(2)}) async-start(), calls=%async_computation.3 | async-start | bytes 1114112 | tf_op jit(solution)/shard_map/all_gather | solution.py:60
  52.3 2.4 %copy-start.7 = (s32[2048,1]{0,1:T(1,128)S(1)}, s32[2048,1]{0,1:T(1,128)}, u32[]{:S(2)}) copy-start(s32[2048,1]{0,1:T(1,128)} %compare_select_fusion.1) | copy-start | bytes 24580
  75.9 2.4 %copy-start.4 = (bf16[16,1024]{1,0:T(8,128)(2,1)S(1)}, bf16[16,1024]{1,0:T(8,128)(2,1)}, u32[]{:S(2)}) copy-start(bf16[16,1024]{1,0:T(8,128)(2,1)} %param.9) | copy-start | bytes 98308
  75.9 2.4 %copy-start.8 = (pred[2048]{0:T(1024)(128)(4,1)S(1)}, pred[2048]{0:T(1024)(128)(4,1)}, u32[]{:S(2)}) copy-start(pred[2048]{0:T(1024)(128)(4,1)} %compare_and_fusion.1) | copy-start | bytes 6148
  83.0 1.0 copy-start
  84.0 2.6 %copy-start.3 = (bf16[16,1024]{1,0:T(8,128)(2,1)S(1)}, bf16[16,1024]{1,0:T(8,128)(2,1)}, u32[]{:S(2)}) copy-start(bf16[16,1024]{1,0:T(8,128)(2,1)} %param.8) | copy-start | bytes 98308
Sparse Core Ops, SparseCore 0:
  151.3 50.7 all-gather.2
